TPU v7x, 256 devices: a whole 4x4x8 slice. The times are simulated.
256 devices in a mesh: space: 16 (over z, x_hi), mrow: 4 (over y), mcol: 4 (over x_lo, core).
Axes of the slice: x: 4 (x_hi: 2, x_lo: 2; x = x_hi * 2 + x_lo), y: 4, z: 8, core: 2. Of those that a mesh axis runs over, the one named last changes fastest.
Arguments:
- deviation: bfloat16 [512, 48, 8192], P('space', None, ('mcol', 'mrow'))
- courant: float32 [2, 8192], P(None, ('mcol', 'mrow')), may hold values from -0.95 to 0.95
- collide: bfloat16 [8192, 8192], P('mrow', ('mcol', 'space'))
- hole_cells: int32 [6144], P('space'), may hold values from -1 to 1535, as said below
- hole_wall: int32 [6144], P('space'), may hold values from 0 to 3
- specular: int32 [4, 8192], replicated, may hold values from 0 to 8191, as said below
- specularity: float32 [4], replicated, may hold values from 0.2 to 0.8
Outputs:
- updated: bfloat16 [512, 48, 8192], P('space', None, ('mrow', 'mcol'))
Inputs may be any that keep to these rules, and one draw needn't show every extreme that they name: `hole_cells`: within one tile the used slots come first and name distinct cells; every tile has at least 96 used slots, some tile has all 384 slots used and some tile has an empty slot. Each row specular[w] is a permutation of the modes; for an outgoing mode i of aligned block e = i // 512, its incoming mode j lies, within j's own aligned block of 512 modes, in the sub-block of 32 modes numbered e, that is (j % 512) // 32 == e.
All inputs are finite; a program needn't handle non-finite values.
Results may differ from a plain program's by a relative error of at most 0.005.
Values may be sent and summed in bfloat16 or wider, within the bound.
A program may use at most 128 MiB of HBM per device.

v0:
```python
import jax
import jax.numpy as jnp
from jax import lax
from jax.sharding import PartitionSpec as P


def extended(x, sides, width):
    for axis, dim in sides:
        size, length = (lax.axis_size(axis), x.shape[dim])
        up = [(i, (i + 1) % size) for i in range(size - 1)]
        down = [(j, i) for i, j in up]
        last = lax.slice_in_dim(x, length - width, length, axis=dim)
        first = lax.slice_in_dim(x, 0, width, axis=dim)
        before = lax.ppermute(last, axis, up)
        after = lax.ppermute(first, axis, down)
        x = jnp.concatenate([before, x, after], axis=dim)
    return x


def upwind(padded, courant):
    field = padded.astype(jnp.float32)
    reach_x = jnp.abs(courant[0])
    reach_y = jnp.abs(courant[1])
    center = field[1:-1]
    upwind_x = jnp.where(courant[0] > 0, field[:-2], field[2:])
    upwind_y = jnp.where(courant[1] > 0, jnp.roll(center, 1, axis=1), jnp.roll(center, -1, axis=1))
    upwind_xy = jnp.where(
        courant[1] > 0, jnp.roll(upwind_x, 1, axis=1), jnp.roll(upwind_x, -1, axis=1)
    )
    result = (1.0 - reach_x) * (1.0 - reach_y) * center + reach_x * (1.0 - reach_y) * upwind_x
    result = result + (1.0 - reach_x) * reach_y * upwind_y + reach_x * reach_y * upwind_xy
    return result.astype(jnp.bfloat16)


def mirror_values(source_rows, wall_tables, one_hot):
    flipped = source_rows.T
    picked = flipped[wall_tables].astype(jnp.float32)
    weights = one_hot.T.astype(jnp.float32)
    chosen = jnp.sum(weights[:, None, :] * picked, axis=0)
    return chosen.T


def reemit(full_rows, wall_tables, one_hot, share):
    mirrored = mirror_values(full_rows, wall_tables, one_hot)
    diffuse = jnp.sum(full_rows.astype(jnp.float32), axis=1) / full_rows.shape[1]
    return (share[:, None] * mirrored + (1.0 - share)[:, None] * diffuse[:, None]).astype(
        jnp.bfloat16
    )


def on_device(deviation, courant, collide, hole_cells, hole_wall, specular, specularity):
    padded = extended(deviation, (("space", 0),), 1)
    read = upwind(padded, courant)
    width_x, width_y, block_len = read.shape
    cell_count = width_x * width_y
    row_groups = lax.axis_size("mrow")
    col_groups = lax.axis_size("mcol")
    is_live = hole_cells >= 0
    safe_ids = jnp.where(is_live, hole_cells, 0)
    target_ids = jnp.where(is_live, hole_cells, cell_count)
    wall_count = specular.shape[0]
    one_hot = hole_wall[:, None] == jnp.arange(wall_count, dtype=jnp.int32)[None, :]
    share = jnp.dot(one_hot.astype(jnp.float32), specularity, precision=lax.Precision.HIGHEST)
    flat_cells = read.reshape(cell_count, block_len)
    start = (lax.axis_index("mcol") * row_groups + lax.axis_index("mrow")) * block_len
    own_table = lax.dynamic_slice_in_dim(specular, start, block_len, 1)
    block_ids = own_table // block_len
    positions = (
        block_ids % row_groups * col_groups + block_ids // row_groups
    ) * block_len + own_table % block_len
    full_rows = lax.all_gather(flat_cells[safe_ids], ("mrow", "mcol"), axis=1, tiled=True)
    emitted = reemit(full_rows, positions, one_hot, share)
    flat_cells = flat_cells.at[target_ids].set(emitted, mode="drop")
    columns = lax.all_gather(
        flat_cells.reshape(width_x, width_y, block_len), "mrow", axis=2, tiled=True
    )
    column_flat = columns.reshape(cell_count, columns.shape[2])
    partial_sums = lax.dot_general(
        column_flat,
        lax.all_gather(collide, "space", axis=1, tiled=True),
        (((1,), (1,)), ((), ())),
        preferred_element_type=jnp.float32,
    )
    summed = lax.psum_scatter(partial_sums, "mcol", scatter_dimension=1, tiled=True)
    return summed.astype(jnp.bfloat16).reshape(width_x, width_y, summed.shape[1])


def solution(mesh):
    in_specs = (
        P("space", None, ("mcol", "mrow")),
        P(None, ("mcol", "mrow")),
        P("mrow", ("mcol", "space")),
        P("space"),
        P("space"),
        P(),
        P(),
    )
    out_specs = P("space", None, ("mrow", "mcol"))
    return jax.shard_map(
        on_device, mesh=mesh, in_specs=in_specs, out_specs=out_specs, check_vma=False
    )
```

profile of v0, /device:TPU:1, one launch (start us, length us, event | category | flops | bytes accessed | tf_op | source)
XLA Modules:
  0.0 448.5 jit_solution(13947178258278800401)
XLA Ops:
  6.5 0.0 copy-start
  6.5 0.0 all-gather.9.cloned.1.call-start
  6.5 0.8 fusion.22
  7.4 5.5 %collective-permute-start = (bf16[1,48,512]{2,1,0:T(8,128)(2,1)S(1)}, bf16[1,48,512]{2,1,0:T(8,128)(2,1)S(1)}, u32[]{:S(2)}, u32[]{:S(2)}) collective-permute-start(bf16[1,48,512]{2,1,0:T(8,128)(2,1)S(1)} %get-tuple-element.15), channel_id=1, source_target_pairs={{0,16},{16,32},{32,48},{48,64},{64,80},{80,96},{96,112},{112,128},... | collective-permute-start | bytes 147464 | tf_op jit(solution)/shard_map/ppermute | solution.py:14
  12.8 1.3 collective-permute-start.1
  14.1 0.8 compare_reduce_fusion
  14.9 0.8 slice_abs_fusion
  15.7 0.7 compare_select_fusion.3
  16.4 0.0 collective-permute-done
  16.4 2.8 collective-permute-done.1
  19.2 1.7 maximum_convert_fusion
  20.9 0.6 slice_select_fusion
  21.5 4.9 %fusion.19 = (f32[32,47,512]{2,1,0:T(8,128)}, f32[32,47,512]{2,1,0:T(8,128)}, f32[32,47,512]{2,1,0:T(8,128)}, f32[32,47,512]{2,1,0:T(8,128)}) fusion(f32[34,48,512]{2,1,0:T(8,128)S(1)} %maximum_convert_fusion, f32[32,48,512]{2,1,0:T(8,128)S(1)} %slice_select_fusion), kind=kLoop, calls=%fused_computation.62 | loop fusion | bytes 24641536 | tf_op jit(solution)/shard_map/jit(_roll_static)/slice | solution.py:26
  26.4 0.1 fusion.21
  26.5 1.1 maximum_convert_fusion.1
  27.6 6.2 %fusion.3 = bf16[32,48,512]{2,1,0:T(8,128)(2,1)S(1)} fusion(f32[34,48,512]{2,1,0:T(8,128)S(1)} %maximum_convert_fusion, f32[32,47,512]{2,1,0:T(8,128)} %get-tuple-element.8, f32[32,1,512]{2,1,0:T(1,128)S(1)} %get-tuple-element.14, f32[32,1,512]{2,1,0:T(1,128)S(1)} %get-tuple-element.13, f32[32,47,512]{2,1,0:T(8,128)} %get-tuple-element.7, ...), kind=kLoop, calls=%fused_computation.9 | loop fusion | flops 11796480 | bytes 23602176 | tf_op jit(solution)/shard_map/convert_element_type | solution.py:32
  33.8 0.0 copy-start.3
  33.9 2.6 gather_fusion
  36.4 0.0 all-gather.9.cloned.1.call-update
  36.5 0.0 all-gather.7.cloned.1.call-start
  36.5 0.7 all-gather.7.cloned.1.call-update
  37.2 0.0 all-gather.5.cloned.1.call-start
  37.3 0.7 fusion.16
  38.0 0.0 copy-done
  38.0 0.0 copy-done.3
  38.0 0.3 convolution_reduce_fusion
  38.4 48.1 %all-gather.9.cloned.1.call-done = bf16[384,8192]{1,0:T(8,128)(2,1)} async-done(((bf16[384,512]{1,0:T(8,128)(2,1)}), bf16[384,8192]{1,0:T(8,128)(2,1)}) %all-gather.9.cloned.1.call-update) | async-done | bytes 6291472 | tf_op jit(solution)/shard_map/all_gather | solution.py:71
  86.5 8.7 %copy.9 = bf16[8192,384]{1,0:T(8,128)(2,1)} copy(bf16[8192,384]{0,1:T(8,128)(2,1)} %bitcast.22) | data formatting | bytes 12582912 | tf_op jit(solution)/shard_map/transpose | solution.py:36
  95.1 10.8 %gather_fusion.1 = bf16[2048,384]{1,0:T(8,128)(2,1)S(1)} fusion(bf16[8192,384]{1,0:T(8,128)(2,1)} %copy.9, s32[2048]{0:T(1024)S(1)} %broadcast_clamp_fusion), kind=kCustom, calls=%fused_computation.1 | custom fusion | bytes 3153920 | tf_op jit(solution)/shard_map/gather | solution.py:37
  105.9 0.3 fusion.6
  106.3 3.7 convert_reduce_fusion
  110.0 0.1 fusion.7
  110.1 0.2 copy.10
  110.3 2.8 scatter_fusion
  113.1 0.0 copy-start.2
  113.1 1.1 copy-done.2
  114.3 0.0 all-gather.5.cloned.1.call-update
  114.3 0.2 reduce-scatter.2.cloned.1.call-start
  114.5 118.4 %all-gather.7.cloned.1.call-done = bf16[2048,2048]{1,0:T(8,128)(2,1)} async-done(((bf16[2048,128]{1,0:T(8,128)(2,1)}), bf16[2048,2048]{1,0:T(8,128)(2,1)}) %all-gather.7.cloned.1.call-update) | async-done | bytes 8388624 | tf_op jit(solution)/shard_map/all_gather | solution.py:80
  232.9 69.9 %all-gather.5.cloned.1.call-done = bf16[32,48,2048]{2,1,0:T(8,128)(2,1)} async-done(((bf16[32,48,512]{2,1,0:T(8,128)(2,1)}), bf16[32,48,2048]{2,1,0:T(8,128)(2,1)}) %all-gather.5.cloned.1.call-update) | async-done | bytes 6291472 | tf_op jit(solution)/shard_map/all_gather | solution.py:74
  302.9 19.0 %fusion.23 = f32[1536,2048]{1,0:T(8,128)} fusion(bf16[1536,2048]{1,0:T(8,128)(2,1)} %bitcast.27, bf16[2048,2048]{1,0:T(8,128)(2,1)} %all-gather.7.cloned.1.call-done), kind=kOutput, calls=%fused_computation.66 | convolution fusion | flops 12884901888 | bytes 27262976 | tf_op jit(solution)/shard_map/dot_general | solution.py:78
  321.9 0.0 reduce-scatter.2.cloned.1.call-update
  321.9 0.0 copy-start.1
  322.0 116.8 %reduce-scatter.2.cloned.1.call-done = f32[1536,512]{1,0:T(8,128)} async-done(((f32[1536,2048]{1,0:T(8,128)}), f32[1536,512]{1,0:T(8,128)}) %reduce-scatter.2.cloned.1.call-update) | async-done | bytes 3145744 | tf_op jit(solution)/shard_map/reduce_scatter | solution.py:84
  438.7 3.2 convert_element_type.36
  442.0 0.0 copy-done.1
  (6 shorter events, 0.0 us)
Async XLA Ops:
  6.5 31.5 %copy-start = (f32[4]{0:T(128)S(1)}, f32[4]{0:T(128)}, u32[]{:S(2)}) copy-start(f32[4]{0:T(128)} %param.13) | copy-start | bytes 52
  6.5 79.9 %all-gather.9.cloned.1.call-start = ((), (), s32[]{:S(2)}) async-start(), calls=%async_computation.4 | async-start | bytes 6684672 | tf_op jit(solution)/shard_map/all_gather | solution.py:71
  7.4 9.0 %collective-permute-start = (bf16[1,48,512]{2,1,0:T(8,128)(2,1)S(1)}, bf16[1,48,512]{2,1,0:T(8,128)(2,1)S(1)}, u32[]{:S(2)}, u32[]{:S(2)}) collective-permute-start(bf16[1,48,512]{2,1,0:T(8,128)(2,1)S(1)} %get-tuple-element.15), channel_id=1, source_target_pairs={{0,16},{16,32},{32,48},{48,64},{64,80},{80,96},{96,112},{112,128},... | collective-permute-start | bytes 147464 | tf_op jit(solution)/shard_map/ppermute | solution.py:14
  12.8 6.3 %collective-permute-start.1 = (bf16[1,48,512]{2,1,0:T(8,128)(2,1)S(1)}, bf16[1,48,512]{2,1,0:T(8,128)(2,1)S(1)}, u32[]{:S(2)}, u32[]{:S(2)}) collective-permute-start(bf16[1,48,512]{2,1,0:T(8,128)(2,1)S(1)} %get-tuple-element.16), channel_id=1, source_target_pairs={{16,0},{32,16},{48,32},{64,48},{80,64},{96,80},{112,96},{128,112},... | collective-permute-start | bytes 147464 | tf_op jit(solution)/shard_map/ppermute | solution.py:15
  33.8 4.2 copy-start.3
  36.5 196.5 %all-gather.7.cloned.1.call-start = ((), (), s32[]{:S(2)}) async-start(), calls=%async_computation.2 | async-start | bytes 8912896 | tf_op jit(solution)/shard_map/all_gather | solution.py:80
  37.2 265.7 %all-gather.5.cloned.1.call-start = ((), (), s32[]{:S(2)}) async-start(), calls=%async_computation.1 | async-start | bytes 7864320 | tf_op jit(solution)/shard_map/all_gather | solution.py:74
  113.1 1.1 copy-start.2
  114.3 324.4 %reduce-scatter.2.cloned.1.call-start = ((), (), s32[]{:S(2)}) async-start(), calls=%async_computation.3 | async-start | bytes 15728640 | tf_op jit(solution)/shard_map/reduce_scatter | solution.py:84
  321.9 120.0 %copy-start.1 = (f32[4]{0:T(128)S(1)}, f32[4]{0:T(128)}, u32[]{:S(2)}) copy-start(f32[4]{0:T(128)} %param.13) | copy-start | bytes 52
Sparse Core Ops, SparseCore 0:
  36.6 49.8 all-gather.8
  88.9 143.9 all-gather.6
  234.8 68.0 all-gather.4
  322.1 116.6 reduce-scatter.1
where the time goes:
time: 449 us; the launch traced here: 448 us
  waiting for transfers between devices  357 us (80%)
  local copies, waits for them, and re-layouts  32.1 us (7%)
  other arithmetic  20 us (4%)
  matrix products  19.3 us (4%)
  between operations  13.3 us (3%)
  starting transfers between devices  7.05 us (2%)
    all_gather x1, waiting for transfers between devices, on_device(): lax.all_gather(collide, 'space', axis=1, tiled=True)  118 us
    reduce_scatter x1, waiting for transfers between devices, on_device(): lax.psum_scatter(partial_sums, 'mcol', scatter_dimension=1, tiled=True)  117 us
    all_gather x1, waiting for transfers between devices, on_device(): lax.all_gather(flat_cells.reshape(width_x, width_y, block_len), 'mrow', a...  69.9 us
    all_gather x1, waiting for transfers between devices, on_device(): lax.all_gather(flat_cells[safe_ids], ('mrow', 'mcol'), axis=1, tiled=True)  48.1 us
    dot_general x1, matrix products, on_device(): lax.dot_general(column_flat, lax.all_gather(collide, 'space', axis=1, til...  19 us
    gather x1, local copies, waits for them, and re-layouts, mirror_values(): picked = flipped[wall_tables].astype(jnp.float32)  10.8 us
  transfers between devices with their start and end apart: 6, of which 5 were waited for; matrix products, arithmetic and copies ran while one was open for 7% of the time, Pallas kernels for 0%

commit v1 on v0

--- a/solution.py
+++ b/solution.py
@@ -71,8 +71,14 @@
     full_rows = lax.all_gather(flat_cells[safe_ids], ("mrow", "mcol"), axis=1, tiled=True)
     emitted = reemit(full_rows, positions, one_hot, share)
     flat_cells = flat_cells.at[target_ids].set(emitted, mode="drop")
-    columns = lax.all_gather(
-        flat_cells.reshape(width_x, width_y, block_len), "mrow", axis=2, tiled=True
+    columns = jnp.concatenate(
+        lax.all_to_all(
+            jnp.stack([flat_cells.reshape(width_x, width_y, block_len)] * lax.axis_size("mrow")),
+            "mrow",
+            0,
+            0,
+        ),
+        axis=2,
     )
     column_flat = columns.reshape(cell_count, columns.shape[2])
     partial_sums = lax.dot_general(

time: 449 us -> 379 us (0.84)
  waiting for transfers between devices: 357 us -> 196 us
  blocking collectives: 0 us -> 74.3 us
  local copies, waits for them, and re-layouts: 32.1 us -> 48.3 us
    all_gather x1, waiting for transfers between devices: 118 us -> 28.3 us  [on_device(): lax.all_gather(collide, 'space', axis=1, tiled=True)]
    all_to_all x0 -> x1, blocking collectives: none -> 74.3 us  [on_device(): lax.all_to_all(jnp.stack([flat_cells.reshape(width_x, width_y, block_len)...]
    all_gather x1 -> x0, waiting for transfers between devices: 69.9 us -> none  [on_device(): lax.all_gather(flat_cells.reshape(width_x, width_y, block_len), 'mrow', a...]
    reshape x0 -> x1, local copies, waits for them, and re-layouts: none -> 8.47 us  [on_device(): jnp.concatenate(lax.all_to_all(jnp.stack([flat_cells.reshape(width_x, wid...]
    unnamed x9 -> x8, local copies, waits for them, and re-layouts: 1.16 us -> 8.14 us
  transfers between devices with their start and end apart: 6 -> 5, of which waited for: 5 -> 4; matrix products, arithmetic and copies ran while one was open for 7% -> 13% of each run, Pallas kernels for 0% -> 0%
where the time goes in v1:
time: 379 us; the launch traced here: 378 us
  waiting for transfers between devices  196 us (52%)
  blocking collectives  74.3 us (20%)
  local copies, waits for them, and re-layouts  48.3 us (13%)
  other arithmetic  20 us (5%)
  matrix products  19.3 us (5%)
  between operations  13.3 us (4%)
  starting transfers between devices  6.83 us (2%)
    reduce_scatter x1, waiting for transfers between devices, on_device(): lax.psum_scatter(partial_sums, 'mcol', scatter_dimension=1, tiled=True)  116 us
    all_to_all x1, blocking collectives, on_device(): lax.all_to_all(jnp.stack([flat_cells.reshape(width_x, width_y, block_len)...  74.3 us
    all_gather x1, waiting for transfers between devices, on_device(): lax.all_gather(flat_cells[safe_ids], ('mrow', 'mcol'), axis=1, tiled=True)  48.1 us
    all_gather x1, waiting for transfers between devices, on_device(): lax.all_gather(collide, 'space', axis=1, tiled=True)  28.3 us
    dot_general x1, matrix products, on_device(): lax.dot_general(column_flat, lax.all_gather(collide, 'space', axis=1, til...  19 us
    gather x1, local copies, waits for them, and re-layouts, mirror_values(): picked = flipped[wall_tables].astype(jnp.float32)  10.8 us
    transpose x1, local copies, waits for them, and re-layouts, mirror_values(): flipped = source_rows.T  8.62 us
    reshape x1, local copies, waits for them, and re-layouts, on_device(): jnp.concatenate(lax.all_to_all(jnp.stack([flat_cells.reshape(width_x, wid...  8.47 us
  transfers between devices with their start and end apart: 5, of which 4 were waited for; matrix products, arithmetic and copies ran while one was open for 13% of the time, Pallas kernels for 0%

profile of v1, /device:TPU:1, one launch (start us, length us, event | category | flops | bytes accessed | tf_op | source)
XLA Modules:
  0.0 377.8 jit_solution(4761398377191515757)
XLA Ops:
  6.5 0.0 copy-start
  6.5 0.0 all-gather.6.cloned.1.call-start
  6.5 0.8 fusion.22
  7.4 5.5 %collective-permute-start = (bf16[1,48,512]{2,1,0:T(8,128)(2,1)S(1)}, bf16[1,48,512]{2,1,0:T(8,128)(2,1)S(1)}, u32[]{:S(2)}, u32[]{:S(2)}) collective-permute-start(bf16[1,48,512]{2,1,0:T(8,128)(2,1)S(1)} %get-tuple-element.15), channel_id=1, source_target_pairs={{0,16},{16,32},{32,48},{48,64},{64,80},{80,96},{96,112},{112,128},... | collective-permute-start | bytes 147464 | tf_op jit(solution)/shard_map/ppermute | solution.py:14
  12.8 1.3 collective-permute-start.1
  14.1 0.8 compare_reduce_fusion
  14.9 0.8 slice_abs_fusion
  15.7 0.7 compare_select_fusion.3
  16.4 0.0 collective-permute-done
  16.4 2.8 collective-permute-done.1
  19.2 1.7 maximum_convert_fusion
  20.9 0.6 slice_select_fusion
  21.5 4.9 %fusion.19 = (f32[32,47,512]{2,1,0:T(8,128)}, f32[32,47,512]{2,1,0:T(8,128)}, f32[32,47,512]{2,1,0:T(8,128)}, f32[32,47,512]{2,1,0:T(8,128)}) fusion(f32[34,48,512]{2,1,0:T(8,128)S(1)} %maximum_convert_fusion, f32[32,48,512]{2,1,0:T(8,128)S(1)} %slice_select_fusion), kind=kLoop, calls=%fused_computation.62 | loop fusion | bytes 24641536 | tf_op jit(solution)/shard_map/jit(_roll_static)/slice | solution.py:26
  26.4 0.1 fusion.21
  26.5 1.1 maximum_convert_fusion.1
  27.6 6.2 %fusion.3 = bf16[32,48,512]{2,1,0:T(8,128)(2,1)S(1)} fusion(f32[34,48,512]{2,1,0:T(8,128)S(1)} %maximum_convert_fusion, f32[32,47,512]{2,1,0:T(8,128)} %get-tuple-element.8, f32[32,1,512]{2,1,0:T(1,128)S(1)} %get-tuple-element.14, f32[32,1,512]{2,1,0:T(1,128)S(1)} %get-tuple-element.13, f32[32,47,512]{2,1,0:T(8,128)} %get-tuple-element.7, ...), kind=kLoop, calls=%fused_computation.9 | loop fusion | flops 11796480 | bytes 23602176 | tf_op jit(solution)/shard_map/convert_element_type | solution.py:32
  33.8 0.0 copy-start.2
  33.8 2.6 gather_fusion
  36.4 0.0 all-gather.6.cloned.1.call-update
  36.4 0.0 all-gather.4.cloned.1.call-start
  36.5 0.7 all-gather.4.cloned.1.call-update
  37.2 0.0 reduce-scatter.2.cloned.1.call-start
  37.2 0.7 fusion.16
  38.0 0.0 copy-done
  38.0 0.0 copy-done.2
  38.0 0.3 convolution_reduce_fusion
  38.4 48.1 %all-gather.6.cloned.1.call-done = bf16[384,8192]{1,0:T(8,128)(2,1)} async-done(((bf16[384,512]{1,0:T(8,128)(2,1)}), bf16[384,8192]{1,0:T(8,128)(2,1)}) %all-gather.6.cloned.1.call-update) | async-done | bytes 6291472 | tf_op jit(solution)/shard_map/all_gather | solution.py:71
  86.5 8.6 %copy.10 = bf16[8192,384]{1,0:T(8,128)(2,1)} copy(bf16[8192,384]{0,1:T(8,128)(2,1)} %bitcast.25) | data formatting | bytes 12582912 | tf_op jit(solution)/shard_map/transpose | solution.py:36
  95.1 10.8 %gather_fusion.1 = bf16[2048,384]{1,0:T(8,128)(2,1)S(1)} fusion(bf16[8192,384]{1,0:T(8,128)(2,1)} %copy.10, s32[2048]{0:T(1024)S(1)} %broadcast_clamp_fusion), kind=kCustom, calls=%fused_computation.1 | custom fusion | bytes 3153920 | tf_op jit(solution)/shard_map/gather | solution.py:37
  105.9 0.3 fusion.6
  106.2 3.7 convert_reduce_fusion
  109.9 0.1 fusion.7
  110.0 0.2 copy.11
  110.2 2.8 scatter_fusion
  113.1 0.8 stack.3
  113.8 74.3 %all_to_all.5 = bf16[4,32,48,512]{3,2,1,0:T(8,128)(2,1)S(1)} all-to-all(bf16[4,32,48,512]{3,2,1,0:T(8,128)(2,1)S(1)} %stack.3), channel_id=1, replica_groups=mesh['space'=16,'mrow'=4,'mcol'=4] {'mrow'}, dimensions={0} | all-to-all | bytes 12582912 | tf_op jit(solution)/shard_map/all_to_all | solution.py:75
  188.2 8.5 %copy.12 = bf16[32,48,4,512]{3,2,1,0:T(4,128)(2,1)} copy(bf16[32,48,4,512]{3,1,0,2:T(8,128)(2,1)S(1)} %bitcast.26) | data formatting | bytes 12582912 | tf_op jit(solution)/shard_map/reshape | solution.py:74
  196.6 8.1 %copy.14 = bf16[192,8,4,512]{3,1,2,0:T(8,128)(2,1)} copy(bf16[192,8,4,512]{3,2,1,0:T(4,128)(2,1)} %bitcast.27) | data formatting | bytes 12582912
  204.7 28.3 %all-gather.4.cloned.1.call-done = bf16[2048,2048]{1,0:T(8,128)(2,1)} async-done(((bf16[2048,128]{1,0:T(8,128)(2,1)}), bf16[2048,2048]{1,0:T(8,128)(2,1)}) %all-gather.4.cloned.1.call-update) | async-done | bytes 8388624 | tf_op jit(solution)/shard_map/all_gather | solution.py:86
  233.0 19.0 %fusion.23 = f32[1536,2048]{1,0:T(8,128)} fusion(bf16[1536,2048]{1,0:T(8,128)(2,1)} %bitcast.28, bf16[2048,2048]{1,0:T(8,128)(2,1)} %all-gather.4.cloned.1.call-done), kind=kOutput, calls=%fused_computation.66 | convolution fusion | flops 12884901888 | bytes 27262976 | tf_op jit(solution)/shard_map/dot_general | solution.py:84
  252.0 0.0 reduce-scatter.2.cloned.1.call-update
  252.1 0.0 copy-start.1
  252.1 116.0 %reduce-scatter.2.cloned.1.call-done = f32[1536,512]{1,0:T(8,128)} async-done(((f32[1536,2048]{1,0:T(8,128)}), f32[1536,512]{1,0:T(8,128)}) %reduce-scatter.2.cloned.1.call-update) | async-done | bytes 3145744 | tf_op jit(solution)/shard_map/reduce_scatter | solution.py:90
  368.1 3.2 convert_element_type.36
  371.3 0.0 copy-done.1
  (6 shorter events, 0.0 us)
Async XLA Ops:
  6.5 31.5 %copy-start = (f32[4]{0:T(128)S(1)}, f32[4]{0:T(128)}, u32[]{:S(2)}) copy-start(f32[4]{0:T(128)} %param.13) | copy-start | bytes 52
  6.5 79.9 %all-gather.6.cloned.1.call-start = ((), (), s32[]{:S(2)}) async-start(), calls=%async_computation.4 | async-start | bytes 6684672 | tf_op jit(solution)/shard_map/all_gather | solution.py:71
  7.4 9.0 %collective-permute-start = (bf16[1,48,512]{2,1,0:T(8,128)(2,1)S(1)}, bf16[1,48,512]{2,1,0:T(8,128)(2,1)S(1)}, u32[]{:S(2)}, u32[]{:S(2)}) collective-permute-start(bf16[1,48,512]{2,1,0:T(8,128)(2,1)S(1)} %get-tuple-element.15), channel_id=1, source_target_pairs={{0,16},{16,32},{32,48},{48,64},{64,80},{80,96},{96,112},{112,128},... | collective-permute-start | bytes 147464 | tf_op jit(solution)/shard_map/ppermute | solution.py:14
  12.8 6.3 %collective-permute-start.1 = (bf16[1,48,512]{2,1,0:T(8,128)(2,1)S(1)}, bf16[1,48,512]{2,1,0:T(8,128)(2,1)S(1)}, u32[]{:S(2)}, u32[]{:S(2)}) collective-permute-start(bf16[1,48,512]{2,1,0:T(8,128)(2,1)S(1)} %get-tuple-element.16), channel_id=1, source_target_pairs={{16,0},{32,16},{48,32},{64,48},{80,64},{96,80},{112,96},{128,112},... | collective-permute-start | bytes 147464 | tf_op jit(solution)/shard_map/ppermute | solution.py:15
  33.8 4.2 %copy-start.2 = (s32[384]{0:T(512)S(1)}, s32[384]{0:T(512)}, u32[]{:S(2)}) copy-start(s32[384]{0:T(512)} %param.11) | copy-start | bytes 4612
  36.4 196.6 %all-gather.4.cloned.1.call-start = ((), (), s32[]{:S(2)}) async-start(), calls=%async_computation.2 | async-start | bytes 8912896 | tf_op jit(solution)/shard_map/all_gather | solution.py:86
  37.2 330.9 %reduce-scatter.2.cloned.1.call-start = ((), (), s32[]{:S(2)}) async-start(), calls=%async_computation.3 | async-start | bytes 15728640 | tf_op jit(solution)/shard_map/reduce_scatter | solution.py:90
  252.1 119.3 %copy-start.1 = (f32[4]{0:T(128)S(1)}, f32[4]{0:T(128)}, u32[]{:S(2)}) copy-start(f32[4]{0:T(128)} %param.13) | copy-start | bytes 52
Sparse Core Ops, SparseCore 0:
  36.6 49.8 all-gather.5
  88.9 144.0 all-gather.3
  252.2 115.8 reduce-scatter.1
